TPU v7x, 32 devices: a whole 2x2x4 slice. The times are simulated.
32 devices in a mesh: member: 4 (over y, x), domain: 8 (over z, core).
Axes of the slice: x: 2, y: 2, z: 4, core: 2. Of those that a mesh axis runs over, the one named last changes fastest.
Arguments:
- ensemble: float32 [80, 4, 3, 16, 2048], P('member', None, None, None, 'domain'), may hold values from -9 to 9
- velocity: float32 [2, 3, 16, 2048], P(None, None, None, 'domain'), may hold values from -0.5 to 0.5
- diffusivity: float32 [4], replicated, may hold values from 0.05 to 0.2
- land_mask: int32 [16, 2048], P(None, 'domain'), may hold values from 0 to 1
- obs_index: int32 [4, 8, 4], replicated, may hold values from 0 to 255, as said below
- obs_owner: int32 [4], replicated, may hold values from 0 to 31, as said below
- obs_value: float32 [4, 8], replicated, may hold values from -4 to 4
- obs_error: float32 [4, 8], replicated, may hold values from 0.2 to 1
Outputs:
- analysis: float32 [80, 4, 3, 16, 2048], P(None, None, None, 'member', 'domain')
Inputs may be any that keep to these rules, and one draw needn't show every extreme that they name: `obs_index`: each observed cell has land_mask 1. The first observation of batch 0 is field 0, level 0 at its block's first row and column; the last observation of batch 3 is field 3, level 2 at its block's last row and column. A device's number is its member index times the number of domain tiles plus its domain index. obs_owner[0] is the first device and obs_owner[3] the last.
All inputs are finite; a program needn't handle non-finite values.
Results may differ from a plain program's by a relative error of at most 0.0001.
Values sent between devices are 32-bit elements; how exact they have to be, the bound alone decides.
No kernel may reach another device: no remote copies, remote signals or barrier semaphores. Data moves between devices by JAX's collectives and lax.ppermute only.
A program may use at most 192 MiB of HBM per device.

v0:
```python
import jax
import jax.numpy as jnp
from jax import lax
from jax.sharding import PartitionSpec as P

LOC_RADIUS = 64


def padded_2(array, sides, width):
    for axis, dim in sides:
        size, length = (lax.axis_size(axis), array.shape[dim])
        up = [(i, (i + 1) % size) for i in range(size)]
        down = [(j, i) for i, j in up]
        last = lax.slice_in_dim(array, length - width, length, axis=dim)
        initial = lax.slice_in_dim(array, 0, width, axis=dim)
        before = lax.ppermute(last, axis, up)
        after = lax.ppermute(initial, axis, down)
        array = jnp.concatenate([before, array, after], axis=dim)
    return array


def broadcast(value, axis, source):
    kept = jnp.where(lax.axis_index(axis) == source, value, 0).astype(value.dtype)
    return lax.psum(kept, axis)


def gaspari(distance, loc_radius):
    scaled = distance / loc_radius
    scaled_safe = jnp.maximum(scaled, 1.0)
    near_part = (
        ((-0.25 * scaled + 0.5) * scaled + 0.625) * scaled - 5.0 / 3.0
    ) * scaled * scaled + 1.0
    far_part = (
        ((((scaled / 12.0 - 0.5) * scaled + 0.625) * scaled + 5.0 / 3.0) * scaled - 5.0) * scaled
        + 4.0
        - 2.0 / (3.0 * scaled_safe)
    )
    return jnp.where(scaled <= 1.0, near_part, jnp.where(scaled < 2.0, far_part, 0.0))


def separation(row_from, col_from, row_to, col_to, grid_width):
    col_gap = jnp.abs(col_from - col_to)
    col_gap = jnp.minimum(col_gap, grid_width - col_gap)
    row_gap = row_from - row_to
    return jnp.sqrt((col_gap * col_gap + row_gap * row_gap).astype(jnp.float32))


def advance(center, col_next, col_prev, row_next, row_prev, flow_u, flow_v, diffuse, wet_part):
    tendency = (
        -flow_u * (col_next - col_prev) * 0.5
        - flow_v * (row_next - row_prev) * 0.5
        + diffuse * (col_next + col_prev + row_next + row_prev - 4.0 * center)
    )
    return wet_part * (center + tendency)


def regroup(member_state):
    return lax.all_to_all(member_state, "member", split_axis=3, concat_axis=0, tiled=True)


def increment_sums(change_flat, wet_cells, levels_total, members):
    per_cell = jnp.sum(change_flat.reshape(members, levels_total, -1), axis=0)
    local_sum = jnp.sum(per_cell * wet_cells[None, :], axis=1)
    return lax.psum((local_sum, jnp.sum(wet_cells)), ("member", "domain"))


def local(ensemble, velocity, diffusivity, land_mask, obs_index, obs_owner, obs_value, obs_error):
    fields = diffusivity.shape[0]
    levels = velocity.shape[1]
    levels_total = fields * levels
    diffuse = diffusivity[None, :, None, None, None]
    domain_count = lax.axis_size("domain")
    wet_all = land_mask.astype(jnp.float32)
    padded = padded_2(ensemble, (("domain", 4),), 1)
    zero_row = jnp.zeros_like(ensemble[:, :, :, :1, :])
    row_next = jnp.concatenate([ensemble[:, :, :, 1:, :], zero_row], axis=3)
    row_prev = jnp.concatenate([zero_row, ensemble[:, :, :, :-1, :]], axis=3)
    stepped = advance(
        ensemble,
        padded[..., 2:],
        padded[..., :-2],
        row_next,
        row_prev,
        velocity[0][None, None],
        velocity[1][None, None],
        diffuse,
        wet_all,
    )
    current = regroup(stepped)
    row_count = current.shape[3]
    first_row = lax.axis_index("member") * row_count
    wet_rows = lax.dynamic_slice_in_dim(wet_all, first_row, row_count, 0)
    members = current.shape[0]
    col_count = current.shape[4]
    grid_width = col_count * domain_count
    loc_radius = float(LOC_RADIUS)
    first_col = lax.axis_index("domain") * col_count
    grid_rows = first_row + jnp.arange(row_count, dtype=jnp.int32)[:, None]
    grid_cols = first_col + jnp.arange(col_count, dtype=jnp.int32)[None, :]
    wet_cells = wet_rows.reshape(-1)
    wet_flat = jnp.broadcast_to(wet_rows[None], (levels_total, row_count, col_count)).reshape(-1)
    flat_state = current.reshape(members, -1)
    spread = jnp.float32(members - 1)
    level_ids = jnp.arange(levels_total, dtype=jnp.int32)
    pending = jnp.zeros((levels_total,), jnp.float32)
    deferred = None
    for batch_num in range(obs_owner.shape[0]):
        obs_slot = obs_index[batch_num]
        owner_dev = obs_owner[batch_num]
        level_of = obs_slot[:, 0] * levels + obs_slot[:, 1]
        position = (level_of * row_count + obs_slot[:, 2]) * col_count + obs_slot[:, 3]
        own_priors = jnp.take(flat_state, position, axis=1).T
        priors = broadcast(own_priors, ("member", "domain"), owner_dev)
        if deferred is not None:
            total_inc, wet_count = increment_sums(deferred, wet_cells, levels_total, members)
            pending = pending + total_inc / (members * wet_count)
        lowered = jnp.sum(
            jnp.where(level_of[:, None] == level_ids[None, :], pending[None, :], 0.0), axis=1
        )
        priors = priors - lowered[:, None]
        obs_rows = owner_dev // domain_count * row_count + obs_slot[:, 2]
        obs_cols = owner_dev % domain_count * col_count + obs_slot[:, 3]
        mutual = gaspari(
            separation(
                obs_rows[:, None],
                obs_cols[:, None],
                obs_rows[None, :],
                obs_cols[None, :],
                grid_width,
            ),
            loc_radius,
        )
        before = flat_state
        for obs_num in range(priors.shape[0]):
            prior_row = priors[obs_num]
            mean_prior = jnp.mean(prior_row)
            anomaly = prior_row - mean_prior
            obs_var = obs_error[batch_num, obs_num]
            denominator = jnp.sum(anomaly * anomaly) / spread + obs_var
            shrink = 1.0 / (1.0 + jnp.sqrt(obs_var / denominator))
            weight = obs_value[batch_num, obs_num] - mean_prior - shrink * anomaly
            taper = gaspari(
                separation(grid_rows, grid_cols, obs_rows[obs_num], obs_cols[obs_num], grid_width),
                loc_radius,
            )
            taper_flat = (
                jnp.broadcast_to(taper[None], (levels_total, row_count, col_count)).reshape(-1)
                * wet_flat
            )
            covariance = jnp.dot(anomaly, flat_state, precision=lax.Precision.HIGHEST)
            kalman = taper_flat * covariance / (spread * denominator)
            flat_state = flat_state + weight[:, None] * kalman[None, :]
            prior_cov = jnp.dot(priors, anomaly, precision=lax.Precision.HIGHEST)
            priors = (
                priors
                + (mutual[obs_num] * prior_cov / (spread * denominator))[:, None] * weight[None, :]
            )
        deferred = flat_state - before
    total_inc, wet_count = increment_sums(deferred, wet_cells, levels_total, members)
    pending = pending + total_inc / (members * wet_count)
    flat_state = (
        flat_state.reshape(members, levels_total, -1)
        - pending[None, :, None] * wet_cells[None, None, :]
    ).reshape(members, -1)
    return flat_state.reshape(members, fields, levels, row_count, col_count)


def solution(mesh):
    in_specs = (
        P("member", None, None, None, "domain"),
        P(None, None, None, "domain"),
        P(),
        P(None, "domain"),
        P(),
        P(),
        P(),
        P(),
    )
    out_specs = P(None, None, None, "member", "domain")
    return jax.shard_map(local, mesh=mesh, in_specs=in_specs, out_specs=out_specs, check_vma=False)
```

profile of v0, /device:TPU:0, one launch (start us, length us, event | category | flops | bytes accessed | tf_op | source)
XLA Modules:
  0.0 1156.5 jit_solution(10798302134221968660)
XLA Ops:
  31.3 8.1 fusion.475
  100.2 12.5 %add_multiply_fusion = f32[20,4,3,16,256]{4,0,2,1,3:T(8,128)} fusion(f32[20,4,3,16,256]{4,0,2,1,3:T(8,128)} %copy.70, f32[20,4,3,15,256]{4,0,2,1,3:T(8,128)} %get-tuple-element.94, f32[20,4,3,15,256]{4,0,2,1,3:T(8,128)} %get-tuple-element.93, f32[20,4,3,16,1]{4,0,2,1,3:T(8,128)S(1)} %copy.62, f32[20,4,3,16,1]{4,0,2,1,3:T(8,128)} %copy.64, f32[4]{0:T(128)} %param.12, ...), kind=kLoop, calls=%fused_computation.6 | loop fusion | flops 17694720 | bytes 15382544 | tf_op jit(solution)/shard_map/mul | solution.py:54
  131.7 38.4 %all-to-all-done = f32[20,4,3,16,256]{4,0,2,1,3:T(8,128)} async-done(((f32[20,4,3,16,256]{4,0,2,1,3:T(8,128)}), f32[20,4,3,16,256]{4,0,2,1,3:T(8,128)}, u32[]{:S(2)}, u32[]{:S(2)}) %all-to-all-start) | async-done | bytes 3932192 | tf_op jit(solution)/shard_map/all_to_all | solution.py:58
  192.2 39.0 %psum.72 = f32[8,80]{1,0:T(8,128)S(1)} all-reduce(f32[8,80]{1,0:T(8,128)S(1)} %fusion.191), channel_id=1, replica_groups=mesh['member'=4,'domain'=8] {'member','domain'}, use_global_device_ids=true, to_apply=%region_0.0 | all-reduce | flops 640 | bytes 5120 | tf_op jit(solution)/shard_map/psum | solution.py:24
  273.1 7.2 multiply_add_fusion.33
  290.2 7.6 multiply_add_fusion.32
  307.8 7.4 multiply_add_fusion.31
  325.0 7.8 multiply_add_fusion.30
  342.9 7.6 multiply_add_fusion.29
  360.4 8.0 multiply_add_fusion.28
  378.4 8.1 multiply_add_fusion.27
  407.8 8.6 subtract_reduce_fusion.3
  419.9 40.7 %all-reduce.4 = (f32[12]{0:T(128)S(1)}, f32[]{:T(128)}, f32[8,80]{1,0:T(8,128)S(1)}) all-reduce(f32[12]{0:T(128)S(1)} %reduce_sum.726, f32[]{:T(128)} %get-tuple-element.126, f32[8,80]{1,0:T(8,128)S(1)} %fusion.190), channel_id=1, replica_groups=mesh['member'=4,'domain'=8] {'member','domain'}, use_global_device_ids=true, to_apply=%region_20.22 | all-reduce | flops 653 | bytes 5224 | tf_op jit(solution)/shard_map/psum | solution.py:64
  604.0 7.4 multiply_add_fusion.18
  621.6 8.7 multiply_add_fusion.17
  636.3 8.0 subtract_reduce_fusion.2
  648.0 40.3 %all-reduce.3 = (f32[12]{0:T(128)S(1)}, f32[8,80]{1,0:T(8,128)S(1)}) all-reduce(f32[12]{0:T(128)S(1)} %reduce_sum.747, f32[8,80]{1,0:T(8,128)S(1)} %fusion.189), channel_id=1, replica_groups=mesh['member'=4,'domain'=8] {'member','domain'}, use_global_device_ids=true, to_apply=%region_43.45 | all-reduce | flops 652 | bytes 5216 | tf_op jit(solution)/shard_map/psum | solution.py:64
  830.5 7.4 multiply_add_fusion.9
  847.9 10.9 multiply_add_fusion.8
  864.9 8.1 subtract_reduce_fusion.1
  876.8 40.4 %all-reduce.2 = (f32[12]{0:T(128)S(1)}, f32[8,80]{1,0:T(8,128)S(1)}) all-reduce(f32[12]{0:T(128)S(1)} %reduce_sum.767, f32[8,80]{1,0:T(8,128)S(1)} %fusion.188), channel_id=1, replica_groups=mesh['member'=4,'domain'=8] {'member','domain'}, use_global_device_ids=true, to_apply=%region_64.66 | all-reduce | flops 652 | bytes 5216 | tf_op jit(solution)/shard_map/psum | solution.py:64
  1061.0 7.3 multiply_add_fusion
  1092.1 40.2 %psum.80 = f32[12]{0:T(128)S(1)} all-reduce(f32[12]{0:T(128)S(1)} %reduce_sum.787), channel_id=1, replica_groups=mesh['member'=4,'domain'=8] {'member','domain'}, use_global_device_ids=true, to_apply=%region_84.86 | all-reduce | flops 12 | bytes 96 | tf_op jit(solution)/shard_map/psum | solution.py:64
  1132.5 23.8 %add_subtract_fusion = f32[80,4,3,4,256]{4,3,2,1,0:T(4,128)} fusion(f32[20,4,3,4,4,256]{5,4,2,1,0,3:T(4,128)} %copy.71, f32[4,3,4,256]{3,2,1,0:T(4,128)S(1)} %broadcast_multiply_fusion, f32[4,3,4,256]{3,2,1,0:T(4,128)S(1)} %mul.7381, f32[80]{0:T(128)S(1)} %get-tuple-element.210, f32[4,3,4,256]{3,2,1,0:T(4,128)S(1)} %mul.7348, f32[80]{0:T(128)S(1)} %fusion.266, ...), kind=kLoop, calls=%fused_computation.21 | loop fusion | flops 63897600 | bytes 9496576 | tf_op jit(solution)/shard_map/sub | solution.py:162
  (656 shorter events, 633.2 us)
Async XLA Ops:
  7.0 87.4 %collective-permute-start = (f32[20,4,3,16,1]{0,3,4,2,1:T(8,128)S(1)}, f32[20,4,3,16,1]{0,3,4,2,1:T(8,128)}, u32[]{:S(2)}, u32[]{:S(2)}) collective-permute-start(f32[20,4,3,16,1]{0,3,4,2,1:T(8,128)S(1)} %copy.76), channel_id=1, source_target_pairs={{1,0},{2,1},{3,2},{4,3},{5,4},{6,5},{7,6},{0,7},{9,8},{10,9},{11,1... | collective-permute-start | bytes 46088 | tf_op jit(solution)/shard_map/ppermute | solution.py:17
  13.6 83.1 %collective-permute-start.1 = (f32[20,4,3,16,1]{0,3,4,2,1:T(8,128)}, f32[20,4,3,16,1]{0,3,4,2,1:T(8,128)}, u32[]{:S(2)}, u32[]{:S(2)}) collective-permute-start(f32[20,4,3,16,1]{0,3,4,2,1:T(8,128)} %copy.77), channel_id=1, source_target_pairs={{0,1},{1,2},{2,3},{3,4},{4,5},{5,6},{6,7},{7,0},{8,9},{9,10},{10,1... | collective-permute-start | bytes 46088 | tf_op jit(solution)/shard_map/ppermute | solution.py:16
  31.3 32.6 %copy-start.28 = (s32[8,4]{0,1:T(4,128)}, s32[8,4]{0,1:T(4,128)S(1)}, u32[]{:S(2)}) copy-start(s32[8,4]{0,1:T(4,128)S(1)} %get-tuple-element.99) | copy-start | bytes 388
  40.1 23.8 %copy-start.18 = (s32[8,1]{0,1:T(1,128)}, s32[8,1]{0,1:T(1,128)S(1)}, u32[]{:S(2)}) copy-start(s32[8,1]{0,1:T(1,128)S(1)} %get-tuple-element.201) | copy-start | bytes 100
  42.0 21.8 %copy-start.20 = (s32[8,1]{0,1:T(1,128)}, s32[8,1]{0,1:T(1,128)S(1)}, u32[]{:S(2)}) copy-start(s32[8,1]{0,1:T(1,128)S(1)} %get-tuple-element.346) | copy-start | bytes 100
  42.0 52.3 %copy-start.22 = (s32[8,1]{0,1:T(1,128)}, s32[8,1]{0,1:T(1,128)S(1)}, u32[]{:S(2)}) copy-start(s32[8,1]{0,1:T(1,128)S(1)} %get-tuple-element.347) | copy-start | bytes 100
  42.0 52.4 %copy-start.24 = (s32[8,1]{0,1:T(1,128)}, s32[8,1]{0,1:T(1,128)S(1)}, u32[]{:S(2)}) copy-start(s32[8,1]{0,1:T(1,128)S(1)} %get-tuple-element.208) | copy-start | bytes 100
  42.0 52.4 %copy-start.26 = (s32[8,1]{0,1:T(1,128)}, s32[8,1]{0,1:T(1,128)S(1)}, u32[]{:S(2)}) copy-start(s32[8,1]{0,1:T(1,128)S(1)} %get-tuple-element.209) | copy-start | bytes 100
  112.7 13.3 %copy-start.29 = (s32[8,4]{0,1:T(4,128)S(1)}, s32[8,4]{0,1:T(4,128)}, u32[]{:S(2)}) copy-start(s32[8,4]{0,1:T(4,128)} %copy-done.28) | copy-start | bytes 388
  112.7 13.3 %copy-start.31 = (s32[8,4]{0,1:T(4,128)S(1)}, s32[8,4]{0,1:T(4,128)}, u32[]{:S(2)}) copy-start(s32[8,4]{0,1:T(4,128)} %copy-done.30) | copy-start | bytes 388
  112.7 14.4 %copy-start.15 = (f32[4,8]{1,0:T(4,128)S(1)}, f32[4,8]{1,0:T(4,128)}, u32[]{:S(2)}) copy-start(f32[4,8]{1,0:T(4,128)} %param.17) | copy-start | bytes 388
  112.7 15.1 %copy-start.16 = (f32[4,8]{1,0:T(4,128)S(1)}, f32[4,8]{1,0:T(4,128)}, u32[]{:S(2)}) copy-start(f32[4,8]{1,0:T(4,128)} %param.16) | copy-start | bytes 388
  112.8 17.3 %copy-start.25 = (s32[8,1]{0,1:T(1,128)S(1)}, s32[8,1]{0,1:T(1,128)}, u32[]{:S(2)}) copy-start(s32[8,1]{0,1:T(1,128)} %copy-done.24) | copy-start | bytes 100
  112.8 17.3 %copy-start.27 = (s32[8,1]{0,1:T(1,128)S(1)}, s32[8,1]{0,1:T(1,128)}, u32[]{:S(2)}) copy-start(s32[8,1]{0,1:T(1,128)} %copy-done.26) | copy-start | bytes 100
  112.8 17.4 %copy-start.21 = (s32[8,1]{0,1:T(1,128)S(1)}, s32[8,1]{0,1:T(1,128)}, u32[]{:S(2)}) copy-start(s32[8,1]{0,1:T(1,128)} %copy-done.20) | copy-start | bytes 100
  112.8 17.4 %copy-start.23 = (s32[8,1]{0,1:T(1,128)S(1)}, s32[8,1]{0,1:T(1,128)}, u32[]{:S(2)}) copy-start(s32[8,1]{0,1:T(1,128)} %copy-done.22) | copy-start | bytes 100
  112.8 17.6 %copy-start.19 = (s32[8,1]{0,1:T(1,128)S(1)}, s32[8,1]{0,1:T(1,128)}, u32[]{:S(2)}) copy-start(s32[8,1]{0,1:T(1,128)} %copy-done.18) | copy-start | bytes 100
  112.8 18.3 %copy-start.36 = (f32[4,256]{1,0:T(4,128)S(1)}, f32[4,256]{1,0:T(4,128)}, u32[]{:S(2)}) copy-start(f32[4,256]{1,0:T(4,128)} %get-tuple-element.103) | copy-start | bytes 12292
  112.8 18.3 %copy-start.35 = (f32[4,256]{1,0:T(4,128)S(1)}, f32[4,256]{1,0:T(4,128)}, u32[]{:S(2)}) copy-start(f32[4,256]{1,0:T(4,128)} %get-tuple-element.15) | copy-start | bytes 12292
  112.8 57.3 %all-to-all-start = ((f32[20,4,3,16,256]{4,0,2,1,3:T(8,128)}), f32[20,4,3,16,256]{4,0,2,1,3:T(8,128)}, u32[]{:S(2)}, u32[]{:S(2)}) async-start(f32[20,4,3,16,256]{4,0,2,1,3:T(8,128)} %add_multiply_fusion), calls=%async_computation | async-start | bytes 9437184 | tf_op jit(solution)/shard_map/all_to_all | solution.py:58
  407.8 53.6 %copy-start.47 = (s32[8]{0:T(128)S(1)}, s32[8]{0:T(128)}, u32[]{:S(2)}) copy-start(s32[8]{0:T(128)} %get-tuple-element.348) | copy-start | bytes 100
  636.3 52.0 %copy-start.46 = (s32[8]{0:T(128)S(1)}, s32[8]{0:T(128)}, u32[]{:S(2)}) copy-start(s32[8]{0:T(128)} %get-tuple-element.202) | copy-start | bytes 100
  864.9 52.2 %copy-start.45 = (s32[8]{0:T(128)S(1)}, s32[8]{0:T(128)}, u32[]{:S(2)}) copy-start(s32[8]{0:T(128)} %get-tuple-element.199) | copy-start | bytes 100
  864.9 57.2 %copy-start.43 = (f32[8,8]{1,0:T(8,128)S(1)}, f32[8,8]{1,0:T(8,128)}, u32[]{:S(2)}) copy-start(f32[8,8]{1,0:T(8,128)} %fusion.166) | copy-start | bytes 772
  (27 other events, 230.9 us)
where the time goes:
time: 1170 us; the launch traced here: 1160 us
  other arithmetic  365 us (31%)
  local copies, waits for them, and re-layouts  289 us (25%)
  blocking collectives  200 us (17%)
  matrix products  134 us (11%)
  between operations  120 us (10%)
  waiting for transfers between devices  38.4 us (3%)
    add x31, other arithmetic, local(): flat_state = flat_state + weight[:, None] * kalman[None, :]  203 us
    add x34, local copies, waits for them, and re-layouts, local(): flat_state = flat_state + weight[:, None] * kalman[None, :]  198 us
    psum x4, blocking collectives, increment_sums(): return lax.psum((local_sum, jnp.sum(wet_cells)), ('member', 'domain'))  162 us
    dot_general x32, matrix products, local(): covariance = jnp.dot(anomaly, flat_state, precision=lax.Precision.HIGHEST)  130 us
    mul x56, other arithmetic, separation(): return jnp.sqrt((col_gap * col_gap + row_gap * row_gap).astype(jnp.float32))  40.8 us
    psum x1, blocking collectives, broadcast(): return lax.psum(kept, axis)  39 us
    all_to_all x1, waiting for transfers between devices, regroup(): lax.all_to_all(member_state, 'member', split_axis=3, concat_axis=0, tiled...  38.4 us
    reduce_sum x4, other arithmetic, increment_sums(): per_cell = jnp.sum(change_flat.reshape(members, levels_total, -1), axis=0)  31.6 us
  transfers between devices with their start and end apart: 3, of which 1 were waited for; matrix products, arithmetic and copies ran while one was open for 7% of the time, Pallas kernels for 0%

commit v1 on v0

--- a/solution.py
+++ b/solution.py
@@ -4,6 +4,12 @@
 from jax.sharding import PartitionSpec as P
 
 LOC_RADIUS = 64
+pools_point = lambda work_x, which_axis: jnp.concatenate(
+    lax.all_to_all(
+        jnp.stack(jnp.split(work_x, lax.axis_size(which_axis), axis=3), axis=0), which_axis, 0, 0
+    ),
+    axis=0,
+)
 
 
 def padded_2(array, sides, width):
@@ -55,7 +61,7 @@
 
 
 def regroup(member_state):
-    return lax.all_to_all(member_state, "member", split_axis=3, concat_axis=0, tiled=True)
+    return pools_point(member_state, "member")
 
 
 def increment_sums(change_flat, wet_cells, levels_total, members):

time: 1170 us -> 1120 us (0.957)
  local copies, waits for them, and re-layouts: 289 us -> 267 us
  other arithmetic: 365 us -> 349 us
    add x31, other arithmetic: 203 us -> 189 us  [local(): flat_state = flat_state + weight[:, None] * kalman[None, :]]
    all_to_all x2 -> x0, local copies, waits for them, and re-layouts: 13.6 us -> none  [regroup(): lax.all_to_all(member_state, 'member', split_axis=3, concat_axis=0, tiled...]
    another operation x0 -> x3, local copies, waits for them, and re-layouts: none -> 12.8 us  [the longest x2 11.7 us: local(): flat_state = current.reshape(members, -1)]
    reshape x2 -> x0, local copies, waits for them, and re-layouts: 11.8 us -> none  [local(): flat_state = current.reshape(members, -1)]
where the time goes in v1:
time: 1120 us; the launch traced here: 1110 us
  other arithmetic  349 us (31%)
  local copies, waits for them, and re-layouts  267 us (24%)
  blocking collectives  201 us (18%)
  matrix products  134 us (12%)
  between operations  120 us (11%)
  waiting for transfers between devices  30.6 us (3%)
    add x34, local copies, waits for them, and re-layouts, local(): flat_state = flat_state + weight[:, None] * kalman[None, :]  198 us
    add x31, other arithmetic, local(): flat_state = flat_state + weight[:, None] * kalman[None, :]  189 us
    psum x4, blocking collectives, increment_sums(): return lax.psum((local_sum, jnp.sum(wet_cells)), ('member', 'domain'))  161 us
    dot_general x32, matrix products, local(): covariance = jnp.dot(anomaly, flat_state, precision=lax.Precision.HIGHEST)  130 us
    mul x56, other arithmetic, separation(): return jnp.sqrt((col_gap * col_gap + row_gap * row_gap).astype(jnp.float32))  40.5 us
    psum x1, blocking collectives, broadcast(): return lax.psum(kept, axis)  39.5 us
    reduce_sum x4, other arithmetic, increment_sums(): per_cell = jnp.sum(change_flat.reshape(members, levels_total, -1), axis=0)  31.1 us
    all_to_all x1, waiting for transfers between devices, lax.all_to_all(jnp.stack(jnp.split(work_x, lax.axis_size(which_axis), axi...  30.6 us
  transfers between devices with their start and end apart: 3, of which 1 were waited for; matrix products, arithmetic and copies ran while one was open for 7% of the time, Pallas kernels for 0%

profile of v1, /device:TPU:0, one launch (start us, length us, event | category | flops | bytes accessed | tf_op | source)
XLA Modules:
  0.0 1110.8 jit_solution(11982151405236438053)
XLA Ops:
  19.8 7.9 fusion.476
  90.6 9.6 add_multiply_fusion
  121.8 30.6 %all-to-all-done = f32[4,20,4,3,4,256]{5,4,3,2,1,0:T(4,128)} async-done(((f32[4,20,4,3,4,256]{5,4,3,2,1,0:T(4,128)}), f32[4,20,4,3,4,256]{5,4,3,2,1,0:T(4,128)}, u32[]{:S(2)}, u32[]{:S(2)}) %all-to-all-start) | async-done | bytes 3932192 | tf_op jit(solution)/shard_map/all_to_all | solution.py:8
  167.5 39.5 %psum.72 = f32[8,80]{1,0:T(8,128)S(1)} all-reduce(f32[8,80]{1,0:T(8,128)S(1)} %fusion.191), channel_id=1, replica_groups=mesh['member'=4,'domain'=8] {'member','domain'}, use_global_device_ids=true, to_apply=%region_0.0 | all-reduce | flops 640 | bytes 5120 | tf_op jit(solution)/shard_map/psum | solution.py:30
  316.0 6.1 add.4295
  326.2 6.8 multiply_add_fusion.28
  342.8 7.3 multiply_add_fusion.27
  371.5 8.1 subtract_reduce_fusion.3
  383.1 40.3 %all-reduce.4 = (f32[12]{0:T(128)S(1)}, f32[]{:T(128)}, f32[8,80]{1,0:T(8,128)S(1)}) all-reduce(f32[12]{0:T(128)S(1)} %reduce_sum.726, f32[]{:T(128)} %get-tuple-element.130, f32[8,80]{1,0:T(8,128)S(1)} %fusion.190), channel_id=1, replica_groups=mesh['member'=4,'domain'=8] {'member','domain'}, use_global_device_ids=true, to_apply=%region_20.22 | all-reduce | flops 653 | bytes 5224 | tf_op jit(solution)/shard_map/psum | solution.py:70
  549.3 6.8 multiply_add_fusion.19
  565.9 7.3 multiply_add_fusion.18
  583.2 8.7 multiply_add_fusion.17
  598.0 8.1 subtract_reduce_fusion.2
  609.7 40.6 %all-reduce.3 = (f32[12]{0:T(128)S(1)}, f32[8,80]{1,0:T(8,128)S(1)}) all-reduce(f32[12]{0:T(128)S(1)} %reduce_sum.747, f32[8,80]{1,0:T(8,128)S(1)} %fusion.189), channel_id=1, replica_groups=mesh['member'=4,'domain'=8] {'member','domain'}, use_global_device_ids=true, to_apply=%region_43.45 | all-reduce | flops 652 | bytes 5216 | tf_op jit(solution)/shard_map/psum | solution.py:70
  775.1 6.8 multiply_add_fusion.10
  791.7 7.4 multiply_add_fusion.9
  809.3 10.9 multiply_add_fusion.8
  826.4 8.1 subtract_reduce_fusion.1
  838.2 40.3 %all-reduce.2 = (f32[12]{0:T(128)S(1)}, f32[8,80]{1,0:T(8,128)S(1)}) all-reduce(f32[12]{0:T(128)S(1)} %reduce_sum.767, f32[8,80]{1,0:T(8,128)S(1)} %fusion.188), channel_id=1, replica_groups=mesh['member'=4,'domain'=8] {'member','domain'}, use_global_device_ids=true, to_apply=%region_64.66 | all-reduce | flops 652 | bytes 5216 | tf_op jit(solution)/shard_map/psum | solution.py:70
  1005.5 6.8 multiply_add_fusion.1
  1022.1 7.3 multiply_add_fusion
  1039.2 7.0 subtract_reduce_fusion
  1046.4 40.0 %psum.80 = f32[12]{0:T(128)S(1)} all-reduce(f32[12]{0:T(128)S(1)} %reduce_sum.787), channel_id=1, replica_groups=mesh['member'=4,'domain'=8] {'member','domain'}, use_global_device_ids=true, to_apply=%region_84.86 | all-reduce | flops 12 | bytes 96 | tf_op jit(solution)/shard_map/psum | solution.py:70
  1086.6 24.0 %add_subtract_fusion = f32[80,4,3,4,256]{4,3,2,1,0:T(4,128)} fusion(f32[4,20,4,3,4,256]{5,4,3,2,1,0:T(4,128)} %all-to-all-done, f32[4,3,4,256]{3,2,1,0:T(4,128)S(1)} %broadcast_multiply_fusion, f32[4,3,4,256]{3,2,1,0:T(4,128)S(1)} %mul.7381, f32[80]{0:T(128)S(1)} %get-tuple-element.214, f32[4,3,4,256]{3,2,1,0:T(4,128)S(1)} %mul.7348, f32[80]{0:T(128)S(1)} %fusion.266, ...), kind=kLoop, calls=%fused_computation.21 | loop fusion | flops 63897600 | bytes 9496576 | tf_op jit(solution)/shard_map/sub | solution.py:168
  (604 shorter events, 604.7 us)
Async XLA Ops:
  4.1 10.3 copy-start.17
  7.6 76.0 %collective-permute-start = (f32[20,4,3,16,1]{0,3,4,2,1:T(8,128)}, f32[20,4,3,16,1]{0,3,4,2,1:T(8,128)}, u32[]{:S(2)}, u32[]{:S(2)}) collective-permute-start(f32[20,4,3,16,1]{0,3,4,2,1:T(8,128)} %copy.32), channel_id=1, source_target_pairs={{1,0},{2,1},{3,2},{4,3},{5,4},{6,5},{7,6},{0,7},{9,8},{10,9},{11,1... | collective-permute-start | bytes 46088 | tf_op jit(solution)/shard_map/ppermute | solution.py:23
  14.1 72.5 %collective-permute-start.1 = (f32[20,4,3,16,1]{0,3,4,2,1:T(8,128)}, f32[20,4,3,16,1]{0,3,4,2,1:T(8,128)}, u32[]{:S(2)}, u32[]{:S(2)}) collective-permute-start(f32[20,4,3,16,1]{0,3,4,2,1:T(8,128)} %copy.33), channel_id=1, source_target_pairs={{0,1},{1,2},{2,3},{3,4},{4,5},{5,6},{6,7},{7,0},{8,9},{9,10},{10,1... | collective-permute-start | bytes 46088 | tf_op jit(solution)/shard_map/ppermute | solution.py:22
  19.8 13.5 %copy-start.16 = (s32[4,8,4]{1,2,0:T(4,128)S(1)}, s32[4,8,4]{1,2,0:T(4,128)}, u32[]{:S(2)}) copy-start(s32[4,8,4]{1,2,0:T(4,128)} %param.14) | copy-start | bytes 1540
  19.8 13.5 %copy-start.9 = (f32[2,3,16,256]{3,2,1,0:T(8,128)S(1)}, f32[2,3,16,256]{3,2,1,0:T(8,128)}, u32[]{:S(2)}) copy-start(f32[2,3,16,256]{3,2,1,0:T(8,128)} %param.11) | copy-start | bytes 294916
  19.8 13.5 %copy-start.10 = (s32[16,256]{1,0:T(8,128)S(1)}, s32[16,256]{1,0:T(8,128)}, u32[]{:S(2)}) copy-start(s32[16,256]{1,0:T(8,128)} %param.13) | copy-start | bytes 49156
  33.3 11.7 %copy-start.14 = (s32[8,4]{0,1:T(4,128)}, s32[8,4]{0,1:T(4,128)S(1)}, u32[]{:S(2)}) copy-start(s32[8,4]{0,1:T(4,128)S(1)} %get-tuple-element.105) | copy-start | bytes 388
  103.8 5.0 copy-start.13
  103.8 12.2 %copy-start.15 = (s32[8,4]{0,1:T(4,128)S(1)}, s32[8,4]{0,1:T(4,128)}, u32[]{:S(2)}) copy-start(s32[8,4]{0,1:T(4,128)} %copy-done.14) | copy-start | bytes 388
  103.8 13.5 %copy-start.7 = (f32[4,8]{1,0:T(4,128)S(1)}, f32[4,8]{1,0:T(4,128)}, u32[]{:S(2)}) copy-start(f32[4,8]{1,0:T(4,128)} %param.17) | copy-start | bytes 388
  103.8 14.2 %copy-start.8 = (f32[4,8]{1,0:T(4,128)S(1)}, f32[4,8]{1,0:T(4,128)}, u32[]{:S(2)}) copy-start(f32[4,8]{1,0:T(4,128)} %param.16) | copy-start | bytes 388
  103.8 17.4 %copy-start.12 = (f32[4,256]{1,0:T(4,128)S(1)}, f32[4,256]{1,0:T(4,128)}, u32[]{:S(2)}) copy-start(f32[4,256]{1,0:T(4,128)} %get-tuple-element.107) | copy-start | bytes 12292
  103.8 17.4 %copy-start.11 = (f32[4,256]{1,0:T(4,128)S(1)}, f32[4,256]{1,0:T(4,128)}, u32[]{:S(2)}) copy-start(f32[4,256]{1,0:T(4,128)} %get-tuple-element.15) | copy-start | bytes 12292
  103.8 48.6 %all-to-all-start = ((f32[4,20,4,3,4,256]{5,4,3,2,1,0:T(4,128)}), f32[4,20,4,3,4,256]{5,4,3,2,1,0:T(4,128)}, u32[]{:S(2)}, u32[]{:S(2)}) async-start(f32[4,20,4,3,4,256]{5,4,3,2,1,0:T(4,128)} %pad_maximum_fusion.2), calls=%async_computation | async-start | bytes 7864320 | tf_op jit(solution)/shard_map/all_to_all | solution.py:8
  371.5 52.7 %copy-start.22 = (s32[8]{0:T(128)S(1)}, s32[8]{0:T(128)}, u32[]{:S(2)}) copy-start(s32[8]{0:T(128)} %get-tuple-element.350) | copy-start | bytes 100
  598.0 52.3 %copy-start.21 = (s32[8]{0:T(128)S(1)}, s32[8]{0:T(128)}, u32[]{:S(2)}) copy-start(s32[8]{0:T(128)} %get-tuple-element.206) | copy-start | bytes 100
  826.3 11.7 %copy-start.19 = (pred[8]{0:T(512)(128)(4,1)S(1)}, pred[8]{0:T(512)(128)(4,1)}, u32[]{:S(2)}) copy-start(pred[8]{0:T(512)(128)(4,1)} %get-tuple-element.31) | copy-start | bytes 28
  826.3 11.8 %copy-start = (f32[12,2,4,128]{3,2,1,0:T(4,128)S(1)}, f32[12,2,4,128]{3,2,1,0:T(4,128)}, u32[]{:S(2)}) copy-start(f32[12,2,4,128]{3,2,1,0:T(4,128)} %broadcast_bitcast_fusion) | copy-start | bytes 147460
  826.3 52.2 %copy-start.20 = (s32[8]{0:T(128)S(1)}, s32[8]{0:T(128)}, u32[]{:S(2)}) copy-start(s32[8]{0:T(128)} %get-tuple-element.203) | copy-start | bytes 100
  826.4 57.1 %copy-start.18 = (f32[8,8]{1,0:T(8,128)S(1)}, f32[8,8]{1,0:T(8,128)}, u32[]{:S(2)}) copy-start(f32[8,8]{1,0:T(8,128)} %fusion.166) | copy-start | bytes 772
  924.5 4.1 copy-start.6
  939.6 4.1 copy-start.5
  955.3 4.1 copy-start.4
  1001.3 4.1 copy-start.1
  (2 other events, 8.1 us)
